TPU v7x, 32 devices: a whole 2x2x4 slice. The times are simulated.
32 devices in a mesh: row: 16 (over z, y, core), col: 2 (over x).
Axes of the slice: x: 2, y: 2, z: 4, core: 2. Of those that a mesh axis runs over, the one named last changes fastest.
Arguments:
- seq: float32 [768, 1024], P('row', 'col'), may hold values from -6 to 6
- query: float32 [768, 1024], P('row', 'col'), may hold values from -24 to 24, as said below
- key: float32 [768, 1024], P('col', 'row'), may hold values from -24 to 24, as said below
- value: float32 [768, 1024], P('col', 'row'), may hold values from -6 to 6
- pair: float32 [768, 768, 128], P('row', 'col'), may hold values from -6 to 6
- w_bias: float32 [128, 32], replicated, may hold values from -0.5 to 0.5
- w_out: float32 [1024, 1024], P(None, 'col'), may hold values from -0.75 to 0.75
- w_left: float32 [1024, 64], P('col'), may hold values from -0.1875 to 0.1875
- w_right: float32 [1024, 64], P('col'), may hold values from -0.1875 to 0.1875
- w_outer: float32 [128, 128], replicated, may hold values from -0.5 to 0.5
- outer_bias: float32 [128], replicated, may hold values from -3 to 3
- w_up: float32 [128, 512], replicated, may hold values from -0.5 to 0.5
- w_down: float32 [512, 128], replicated, may hold values from -0.25 to 0.25
Outputs:
- seq_new: float32 [768, 1024], P('row', 'col')
- pair_new: float32 [768, 768, 128], P('row', 'col')
Inputs may be any that keep to these rules, and one draw needn't show every extreme that they name: `query`: Head-major queries of order one; some residues may be much larger. `key`: Head-major keys of order one; some residues may be much larger.
All inputs are finite; a program needn't handle non-finite values.
Results may differ from a plain program's by a relative error of at most 0.0003.
Values sent between devices are 32-bit elements; how exact they have to be, the bound alone decides.
A program may use at most 128 MiB of HBM per device.

v0:
```python
import jax
import jax.numpy as jnp
from jax import lax
from jax.sharding import PartitionSpec as P

HIGH = lax.Precision.HIGHEST


def merged(x, axis, combine):
    everything = jax.tree.map(lambda part: lax.all_gather(part, axis), x)
    leading = jax.tree.map(lambda part: part[0], everything)

    def hop(k, so_far):
        return combine(so_far, jax.tree.map(lambda part: part[k], everything))

    return lax.fori_loop(1, lax.axis_size(axis), hop, leading)


def channel_norm(x):
    centre = x - jnp.mean(x, axis=-1, keepdims=True)
    return centre * lax.rsqrt(jnp.mean(centre * centre, axis=-1, keepdims=True) + 1e-05)


def combine(first, second):
    top = jnp.maximum(first[0], second[0])
    scale_one = jnp.exp(first[0] - top)
    scale_two = jnp.exp(second[0] - top)
    totals = first[1] * scale_one + second[1] * scale_two
    weighted = first[2] * scale_one[..., None] + second[2] * scale_two[..., None]
    return (top, totals, weighted)


def partial_softmax(q_heads, k_heads, v_heads, bias, scale):
    scores = jnp.einsum("ihd,jhd->ihj", q_heads, k_heads, precision=HIGH) * scale + bias
    top = jnp.max(scores, axis=2)
    expo = jnp.exp(scores - top[..., None])
    totals = jnp.sum(expo, axis=2)
    weighted = jnp.einsum("ihj,jhd->ihd", expo, v_heads, precision=HIGH)
    return (top, totals, weighted)


def per_device(
    seq, query, key, value, pair, w_bias, w_out, w_left, w_right, w_outer, outer_bias, w_up, w_down
):
    rows_here = pair.shape[0]
    cols_here = pair.shape[1]
    channels = pair.shape[2]
    heads = w_bias.shape[1]
    width = w_out.shape[0]
    head_dim = width // heads
    proj_width = w_left.shape[1]
    scale = 1.0 / jnp.sqrt(jnp.float32(head_dim))
    bias = jnp.einsum("ijc,ch->ihj", channel_norm(pair), w_bias, precision=HIGH)
    queries = lax.all_gather(query, "col", axis=1, tiled=True)
    keys_all, values_all = (
        lax.all_gather(key, "row", axis=1, tiled=True),
        lax.all_gather(value, "row", axis=1, tiled=True),
    )
    parts = partial_softmax(
        queries.reshape(rows_here, heads, head_dim),
        keys_all.reshape(cols_here, heads, head_dim),
        values_all.reshape(cols_here, heads, head_dim),
        bias,
        scale,
    )
    top, totals, weighted = merged(parts, "col", combine)
    attn = (weighted / totals[..., None]).reshape(rows_here, width)
    seq_new = seq + jnp.dot(attn, w_out, precision=HIGH)
    sum_value, sum_square = lax.psum(
        (jnp.sum(seq_new, axis=1), jnp.sum(seq_new * seq_new, axis=1)), "col"
    )
    mean_value = (sum_value / width)[:, None]
    mean_square = (sum_square / width)[:, None]
    seq_norm = (seq_new - mean_value) * lax.rsqrt(mean_square - mean_value * mean_value + 1e-05)
    left_part = jnp.dot(seq_norm, w_left, precision=HIGH)
    right_part = jnp.dot(seq_norm, w_right, precision=HIGH)
    left, right = lax.psum((left_part, right_part), "col")
    right_every = lax.all_gather(right, "row", axis=0, tiled=True)
    start = lax.axis_index("col") * cols_here
    right_block = lax.dynamic_slice_in_dim(right_every, start, cols_here, 0)
    w_prod = w_outer[:proj_width]
    w_diff = w_outer[proj_width:]
    table = right_block[:, :, None] * w_prod[None, :, :]
    left_diff = jnp.dot(left, w_diff, precision=HIGH)
    right_diff = jnp.dot(right_block, w_diff, precision=HIGH)
    outer = (
        jnp.einsum("ip,jpc->ijc", left, table, precision=HIGH)
        + left_diff[:, None, :]
        - right_diff[None, :, :]
        + outer_bias
    )
    pair_mid = pair + outer
    flat = pair_mid.reshape(rows_here * cols_here, channels)
    hidden_act = jax.nn.relu(jnp.dot(channel_norm(flat), w_up, precision=HIGH))
    pair_new = flat + jnp.dot(hidden_act, w_down, precision=HIGH)
    return (seq_new, pair_new.reshape(rows_here, cols_here, channels))


def solution(mesh):
    in_specs = (
        P("row", "col"),
        P("row", "col"),
        P("col", "row"),
        P("col", "row"),
        P("row", "col", None),
        P(),
        P(None, "col"),
        P("col", None),
        P("col", None),
        P(),
        P(),
        P(),
        P(),
    )
    out_specs = (P("row", "col"), P("row", "col", None))
    return jax.shard_map(
        per_device, mesh=mesh, in_specs=in_specs, out_specs=out_specs, check_vma=False
    )
```

profile of v0, /device:TPU:0, one launch (start us, length us, event | category | flops | bytes accessed | tf_op | source)
XLA Modules:
  0.0 295.0 jit_solution(9783816739350070599)
XLA Ops:
  7.2 0.0 copy-start
  7.2 0.0 all-gather.8.cloned.1.call-start
  7.2 0.7 all-gather.8.cloned.1.call-update
  7.9 0.0 all-gather.10.cloned.1.call-start
  8.0 0.7 all-gather.10.cloned.1.call-update
  8.7 6.7 %all_gather.31 = f32[48,1024]{1,0:T(8,128)S(1)} all-gather(f32[48,512]{1,0:T(8,128)} %param.14), channel_id=1, replica_groups=mesh['row'=16,'col'=2] {'col'}, dimensions={1}, use_global_device_ids=true | all-gather | bytes 294912 | tf_op jit(solution)/shard_map/all_gather | solution.py:54
  15.4 0.2 copy.49
  15.6 0.0 copy-start.7
  15.6 6.2 %reduce_sum.63 = f32[48,384]{1,0:T(8,128)S(1)} reduce(f32[48,384,128]{2,1,0:T(8,128)} %param.17, f32[]{:T(128)} %constant.13.clone.1), dimensions={2}, to_apply=%region_0.0 | reduce | flops 2340864 | bytes 9510916 | tf_op jit(solution)/shard_map/reduce_sum | solution.py:20
  21.8 7.7 %multiply_reduce_fusion.1 = f32[48,384]{1,0:T(8,128)S(1)} fusion(f32[48,384,128]{2,1,0:T(8,128)} %param.17, f32[48,384]{1,0:T(8,128)S(1)} %broadcast_multiply_fusion.1), kind=kLoop, calls=%fused_computation.12 | loop fusion | flops 7059456 | bytes 9584640 | tf_op jit(solution)/shard_map/reduce_sum | solution.py:21
  29.5 0.0 copy-done.7
  29.5 15.9 %fusion.9 = f32[48,384,32]{1,2,0:T(8,128)} fusion(f32[48,384,128]{2,1,0:T(8,128)} %param.17, f32[48,384]{1,0:T(8,128)S(1)} %add_rsqrt_fusion.1, f32[48,384]{1,0:T(8,128)S(1)} %broadcast_multiply_fusion.1, f32[128,32]{0,1:T(8,128)S(1)} %copy-done.7), kind=kOutput, calls=%fused_computation.10 | convolution fusion | flops 910688256 | bytes 11960320 | tf_op jit(solution)/shard_map/ijc,ch->ihj/dot_general | solution.py:53
  45.4 7.2 %all-gather.8.cloned.1.call-done = f32[384,1024]{0,1:T(8,128)} async-done(((f32[384,64]{0,1:T(8,128)}), f32[384,1024]{0,1:T(8,128)}) %all-gather.8.cloned.1.call-update) | async-done | bytes 1572880 | tf_op jit(solution)/shard_map/all_gather | solution.py:56
  52.6 5.7 %fusion.45 = (f32[48,32]{0,1:T(8,128)S(1)}, f32[48,32,384]{2,0,1:T(8,128)S(1)}) fusion(f32[48,384,32]{1,2,0:T(8,128)} %fusion.9, f32[384,32,32]{0,2,1:T(8,128)} %bitcast.72, f32[48,32,32]{0,2,1:T(8,128)S(1)} %bitcast.70), kind=kOutput, calls=%fused_computation.63 | convolution fusion | flops 228260352 | bytes 6494208 | tf_op jit(solution)/shard_map/ihd,jhd->ihj/dot_general | solution.py:34
  58.3 0.0 copy-start.4
  58.3 0.0 slice-start.6
  58.3 1.4 copy-done.2
  59.7 0.8 fusion.18
  60.5 32.7 %all-gather.10.cloned.1.call-done = f32[384,1024]{0,1:T(8,128)} async-done(((f32[384,64]{0,1:T(8,128)}), f32[384,1024]{0,1:T(8,128)}) %all-gather.10.cloned.1.call-update) | async-done | bytes 1572880 | tf_op jit(solution)/shard_map/all_gather | solution.py:57
  93.3 5.1 %fusion.20 = f32[48,32,32]{0,2,1:T(8,128)S(1)} fusion(f32[384,32,32]{0,2,1:T(8,128)} %bitcast.71, f32[48,32,384]{2,0,1:T(8,128)} %copy-done.2, f32[48,32]{0,1:T(8,128)S(1)} %get-tuple-element.37), kind=kOutput, calls=%fused_computation.22 | convolution fusion | flops 227082240 | bytes 4134912 | tf_op jit(solution)/shard_map/ihj,jhd->ihd/dot_general | solution.py:38
  98.3 4.4 %all-gather.3 = f32[2,48,32]{1,2,0:T(8,128)S(1)} all-gather(f32[1,48,32]{1,2,0:T(8,128)S(1)} %bitcast.73), channel_id=3, replica_groups=mesh['row'=16,'col'=2] {'col'}, dimensions={0}, use_global_device_ids=true | all-gather | bytes 18432 | tf_op jit(solution)/shard_map/all_gather | solution.py:10
  102.8 4.4 %all-gather.4 = f32[2,48,32]{1,2,0:T(8,128)S(1)} all-gather(f32[1,48,32]{1,2,0:T(8,128)S(1)} %bitcast.74), channel_id=4, replica_groups=mesh['row'=16,'col'=2] {'col'}, dimensions={0}, use_global_device_ids=true | all-gather | bytes 18432 | tf_op jit(solution)/shard_map/all_gather | solution.py:10
  107.2 0.1 copy.54
  107.2 0.1 copy.52
  107.3 0.7 copy.53
  108.0 0.7 copy.51
  108.7 0.0 copy-start.8
  108.7 18.0 %all-gather = f32[96,32,32]{2,1,0:T(8,128)S(1)} all-gather(f32[48,32,32]{2,1,0:T(8,128)S(1)} %copy.51), channel_id=2, replica_groups=mesh['row'=16,'col'=2] {'col'}, dimensions={0}, use_global_device_ids=true | all-gather | bytes 589824 | tf_op jit(solution)/shard_map/all_gather | solution.py:10
  126.8 2.0 fusion.23
  128.8 0.4 reshape.150
  129.2 0.0 copy-done
  129.2 2.3 fusion.42
  131.5 0.0 copy-start.3
  131.5 4.9 %all-reduce.1 = (f32[48]{0:T(128)S(1)}, f32[48]{0:T(128)S(1)}) all-reduce(f32[48]{0:T(128)S(1)} %get-tuple-element.19, f32[48]{0:T(128)S(1)} %get-tuple-element.18), channel_id=1, replica_groups=mesh['row'=16,'col'=2] {'col'}, use_global_device_ids=true, to_apply=%region_7.0 | all-reduce | flops 96 | bytes 768 | tf_op jit(solution)/shard_map/psum | solution.py:69
  136.5 1.2 fusion.24
  137.7 1.2 fusion.25
  138.9 8.6 %all-reduce = (f32[48,64]{1,0:T(8,128)S(1)}, f32[48,64]{1,0:T(8,128)S(1)}) all-reduce(f32[48,64]{1,0:T(8,128)S(1)} %fusion.24, f32[48,64]{1,0:T(8,128)S(1)} %fusion.25), channel_id=1, replica_groups=mesh['row'=16,'col'=2] {'col'}, use_global_device_ids=true, to_apply=%region_9.0 | all-reduce | flops 6144 | bytes 49152 | tf_op jit(solution)/shard_map/psum | solution.py:77
  147.5 0.0 copy-done.4
  147.5 0.2 fusion.32
  147.6 20.2 %all_gather.39 = f32[768,64]{1,0:T(8,128)S(1)} all-gather(f32[48,64]{1,0:T(8,128)S(1)} %get-tuple-element.20), channel_id=1, replica_groups=mesh['row'=16,'col'=2] {'row'}, dimensions={0}, use_global_device_ids=true | all-gather | bytes 208896 | tf_op jit(solution)/shard_map/all_gather | solution.py:78
  167.9 0.3 fusion.30
  168.2 22.6 %fusion.46 = (f32[48,384]{0,1:T(8,128)S(1)}, f32[48,384,128]{2,0,1:T(8,128)}) fusion(f32[128]{0:T(128)S(1)} %copy-done.8, f32[384,128]{1,0:T(8,128)S(1)} %fusion.30, f32[48,128]{1,0:T(8,128)S(1)} %fusion.32, f32[64,128]{1,0:T(8,128)S(1)} %slice-done.6, f32[384,64]{1,0:T(8,128)S(1)} %constant_dynamic-slice_fusion, f32[48,64]{1,0:T(8,128)S(1)} %get-tuple-element.21, ...), kind=kOutput, calls=%fused_computation.64 | convolution fusion | flops 1826863104 | bytes 19313152 | tf_op jit(solution)/shard_map/ip,jpc->ijc/dot_general | solution.py:87
  190.8 0.1 copy.57
  190.9 0.0 slice-start
  190.9 0.1 copy.58
  191.1 0.0 slice-start.1
  191.1 0.0 slice-start.2
  191.1 10.5 %copy.56 = f32[48,384,128]{2,1,0:T(8,128)} copy(f32[48,384,128]{2,0,1:T(8,128)} %get-tuple-element.41) | data formatting | bytes 18874368 | tf_op jit(solution)/shard_map/add | solution.py:92
  201.5 0.0 slice-done
  201.5 0.0 slice-done.2
  201.6 5.4 %multiply_reduce_fusion = f32[48,384]{0,1:T(8,128)S(1)} fusion(f32[48,384,128]{2,0,1:T(8,128)S(1)} %bitcast.65, f32[48,384]{0,1:T(8,128)S(1)} %copy.58), kind=kLoop, calls=%fused_computation.9 | loop fusion | flops 7059456 | bytes 9584640 | tf_op jit(solution)/shard_map/reduce_sum | solution.py:21
  207.0 0.1 copy.59
  207.1 0.0 copy-start.5
  207.2 0.0 slice-start.3
  207.2 11.4 %fusion.8 = f32[18432,128]{1,0:T(8,128)S(1)} fusion(f32[48,384,128]{2,1,0:T(8,128)} %copy.56, f32[18432]{0:T(1024)S(1)} %rsqrt.26, f32[18432]{0:T(1024)S(1)} %div.39), kind=kLoop, calls=%fused_computation.7 | loop fusion | flops 4718592 | bytes 19021824 | tf_op jit(solution)/shard_map/mul | solution.py:21
  218.6 0.0 copy-done.5
  218.6 0.0 slice-start.4
  218.6 0.0 slice-start.5
  218.6 0.0 copy-start.6
  218.6 33.8 %fusion.47 = f32[18432,512]{1,0:T(8,128)} fusion(f32[18432,128]{1,0:T(8,128)S(1)} %fusion.8, f32[128,512]{1,0:T(8,128)S(1)} %copy-done.5), kind=kOutput, calls=%fused_computation.65 | convolution fusion | flops 14495514624 | bytes 47448064 | tf_op jit(solution)/shard_map/dot_general | solution.py:94
  252.4 0.0 slice-done.5
  252.4 0.0 copy-done.6
  252.4 0.0 copy-start.1
  252.4 35.4 %fusion.2 = f32[18432,128]{1,0:T(8,128)} fusion(f32[18432,128]{1,0:T(8,128)S(1)} %bitcast.68, f32[512,128]{1,0:T(8,128)S(1)} %copy-done.6, f32[18432,512]{1,0:T(8,128)} %fusion.47), kind=kOutput, calls=%fused_computation.2 | convolution fusion | flops 14507311104 | bytes 56885248 | tf_op jit(solution)/shard_map/dot_general | solution.py:95
  (19 shorter events, 0.1 us)
Async XLA Ops:
  7.2 122.0 %copy-start = (f32[1024,512]{1,0:T(8,128)S(1)}, f32[1024,512]{1,0:T(8,128)}, u32[]{:S(2)}) copy-start(f32[1024,512]{1,0:T(8,128)} %param.19) | copy-start | bytes 6291460
  7.2 45.5 %all-gather.8.cloned.1.call-start = ((), (), s32[]{:S(2)}) async-start(), calls=%async_computation | async-start | bytes 1671168 | tf_op jit(solution)/shard_map/all_gather | solution.py:56
  7.9 85.3 %all-gather.10.cloned.1.call-start = ((), (), s32[]{:S(2)}) async-start(), calls=%async_computation.1 | async-start | bytes 1671168 | tf_op jit(solution)/shard_map/all_gather | solution.py:57
  15.6 14.0 %copy-start.7 = (f32[128,32]{0,1:T(8,128)S(1)}, f32[128,32]{0,1:T(8,128)}, u32[]{:S(2)}) copy-start(f32[128,32]{0,1:T(8,128)} %param.18) | copy-start | bytes 49156
  58.3 1.4 copy-start.2
  58.3 89.2 %copy-start.4 = (f32[128,128]{1,0:T(8,128)S(1)}, f32[128,128]{1,0:T(8,128)}, u32[]{:S(2)}) copy-start(f32[128,128]{1,0:T(8,128)} %param.22) | copy-start | bytes 196612
  58.3 109.8 %slice-start.6 = ((f32[128,128]{1,0:T(8,128)}), f32[64,128]{1,0:T(8,128)S(1)}, s32[]{:S(2)}) async-start(f32[128,128]{1,0:T(8,128)} %param.22), calls=%async_computation.8 | async-start | bytes 65536 | tf_op jit(solution)/shard_map/slice | solution.py:81
  108.7 59.4 %copy-start.8 = (f32[128]{0:T(128)S(1)}, f32[128]{0:T(128)}, u32[]{:S(2)}) copy-start(f32[128]{0:T(128)} %param.23) | copy-start | bytes 1540
  131.5 59.3 %copy-start.3 = (f32[48,512]{1,0:T(8,128)}, f32[48,512]{1,0:T(8,128)S(1)}, u32[]{:S(2)}) copy-start(f32[48,512]{1,0:T(8,128)S(1)} %get-tuple-element.39) | copy-start | bytes 294916
  190.9 10.6 %slice-start = ((s8[9437184]{0:T(1024)(128)(4,1)}), s8[1048576]{0:T(1024)(128)(4,1)S(1)}, s32[]{:S(2)}) async-start(s8[9437184]{0:T(1024)(128)(4,1)} %bitcast.64), calls=%async_computation.2 | async-start | bytes 2097152
  191.1 10.5 %slice-start.1 = ((s8[9437184]{0:T(1024)(128)(4,1)}), s8[4194304]{0:T(1024)(128)(4,1)S(1)}, s32[]{:S(2)}) async-start(s8[9437184]{0:T(1024)(128)(4,1)} %bitcast.64), calls=%async_computation.3 | async-start | bytes 8388608
  191.1 10.5 %slice-start.2 = ((s8[9437184]{0:T(1024)(128)(4,1)}), s8[4194304]{0:T(1024)(128)(4,1)S(1)}, s32[]{:S(2)}) async-start(s8[9437184]{0:T(1024)(128)(4,1)} %bitcast.64), calls=%async_computation.4 | async-start | bytes 8388608
  207.1 11.4 %copy-start.5 = (f32[128,512]{1,0:T(8,128)S(1)}, f32[128,512]{1,0:T(8,128)}, u32[]{:S(2)}) copy-start(f32[128,512]{1,0:T(8,128)} %param.24) | copy-start | bytes 786436
  207.2 45.3 %slice-start.3 = ((s8[9437184]{0:T(1024)(128)(4,1)}), s8[4194304]{0:T(1024)(128)(4,1)S(1)}, s32[]{:S(2)}) async-start(s8[9437184]{0:T(1024)(128)(4,1)} %bitcast.66), calls=%async_computation.5 | async-start | bytes 8388608
  218.6 33.8 %slice-start.4 = ((s8[9437184]{0:T(1024)(128)(4,1)}), s8[4194304]{0:T(1024)(128)(4,1)S(1)}, s32[]{:S(2)}) async-start(s8[9437184]{0:T(1024)(128)(4,1)} %bitcast.66), calls=%async_computation.6 | async-start | bytes 8388608
  218.6 33.8 %slice-start.5 = ((s8[9437184]{0:T(1024)(128)(4,1)}), s8[1048576]{0:T(1024)(128)(4,1)S(1)}, s32[]{:S(2)}) async-start(s8[9437184]{0:T(1024)(128)(4,1)} %bitcast.66), calls=%async_computation.7 | async-start | bytes 2097152
  218.6 33.8 %copy-start.6 = (f32[512,128]{1,0:T(8,128)S(1)}, f32[512,128]{1,0:T(8,128)}, u32[]{:S(2)}) copy-start(f32[512,128]{1,0:T(8,128)} %param.25) | copy-start | bytes 786436
  252.4 35.5 %copy-start.1 = (f32[1024,512]{1,0:T(8,128)S(1)}, f32[1024,512]{1,0:T(8,128)}, u32[]{:S(2)}) copy-start(f32[1024,512]{1,0:T(8,128)} %param.19) | copy-start | bytes 6291460
Sparse Core Ops, SparseCore 0:
  10.3 42.3 all-gather.7
  54.9 38.2 all-gather.9
where the time goes:
time: 298 us; the launch traced here: 295 us
  matrix products  124 us (42%)
  blocking collectives  67.2 us (23%)
  waiting for transfers between devices  41.3 us (14%)
  other arithmetic  33.6 us (11%)
  between operations  14.6 us (5%)
  local copies, waits for them, and re-layouts  14.4 us (5%)
    dot_general x1, matrix products, per_device(): pair_new = flat + jnp.dot(hidden_act, w_down, precision=HIGH)  35.4 us
    dot_general x1, matrix products, per_device(): hidden_act = jax.nn.relu(jnp.dot(channel_norm(flat), w_up, precision=HIGH))  33.8 us
    all_gather x1, waiting for transfers between devices, per_device(): lax.all_gather(value, 'row', axis=1, tiled=True)  32.7 us
    all_gather x3, blocking collectives, merged(): everything = jax.tree.map(lambda part: lax.all_gather(part, axis), x)  26.8 us
    dot_general x1, matrix products, per_device(): jnp.einsum('ip,jpc->ijc', left, table, precision=HIGH)  22.6 us
    all_gather x1, blocking collectives, per_device(): right_every = lax.all_gather(right, 'row', axis=0, tiled=True)  20.2 us
    dot_general x1, matrix products, per_device(): bias = jnp.einsum('ijc,ch->ihj', channel_norm(pair), w_bias, precision=HIGH)  15.9 us
    reduce_sum x2, other arithmetic, channel_norm(): jnp.mean(centre * centre, axis=-1, keepdims=True) + 1e-05  13.1 us
  transfers between devices with their start and end apart: 2, of which 2 were waited for; matrix products, arithmetic and copies ran while one was open for 12% of the time, Pallas kernels for 0%

commit v1 on v0

--- a/solution.py
+++ b/solution.py
@@ -54,7 +54,9 @@
     queries = lax.all_gather(query, "col", axis=1, tiled=True)
     keys_all, values_all = (
         lax.all_gather(key, "row", axis=1, tiled=True),
-        lax.all_gather(value, "row", axis=1, tiled=True),
+        jnp.concatenate(
+            lax.all_to_all(jnp.stack([value] * lax.axis_size("row")), "row", 0, 0), axis=1
+        ),
     )
     parts = partial_softmax(
         queries.reshape(rows_here, heads, head_dim),

time: 298 us -> 282 us (0.946)
  waiting for transfers between devices: 41.3 us -> 14.9 us
  starting transfers between devices: 0.08 us -> 7.5 us
    all_gather x1 -> x0, waiting for transfers between devices: 32.7 us -> none  [per_device(): lax.all_gather(value, 'row', axis=1, tiled=True)]
    all_to_all x0 -> x1, starting transfers between devices: none -> 7.46 us  [per_device(): lax.all_to_all(jnp.stack([value] * lax.axis_size('row')), 'row', 0, 0)]
    all_gather x1, waiting for transfers between devices: 7.2 us -> 14.3 us  [per_device(): lax.all_gather(key, 'row', axis=1, tiled=True)]
  transfers between devices with their start and end apart: 2 -> 2, of which waited for: 2 -> 1; matrix products, arithmetic and copies ran while one was open for 12% -> 14% of each run, Pallas kernels for 0% -> 0%
where the time goes in v1:
time: 282 us; the launch traced here: 279 us
  matrix products  124 us (44%)
  blocking collectives  68.1 us (24%)
  other arithmetic  33.6 us (12%)
  local copies, waits for them, and re-layouts  16.6 us (6%)
  waiting for transfers between devices  14.9 us (5%)
  between operations  14.7 us (5%)
  starting transfers between devices  7.5 us (3%)
    dot_general x1, matrix products, per_device(): pair_new = flat + jnp.dot(hidden_act, w_down, precision=HIGH)  35.4 us
    dot_general x1, matrix products, per_device(): hidden_act = jax.nn.relu(jnp.dot(channel_norm(flat), w_up, precision=HIGH))  33.8 us
    all_gather x3, blocking collectives, merged(): everything = jax.tree.map(lambda part: lax.all_gather(part, axis), x)  26.8 us
    dot_general x1, matrix products, per_device(): jnp.einsum('ip,jpc->ijc', left, table, precision=HIGH)  22.6 us
    all_gather x1, blocking collectives, per_device(): right_every = lax.all_gather(right, 'row', axis=0, tiled=True)  21.9 us
    dot_general x1, matrix products, per_device(): bias = jnp.einsum('ijc,ch->ihj', channel_norm(pair), w_bias, precision=HIGH)  15.9 us
    all_gather x1, waiting for transfers between devices, per_device(): lax.all_gather(key, 'row', axis=1, tiled=True)  14.3 us
    reduce_sum x2, other arithmetic, channel_norm(): jnp.mean(centre * centre, axis=-1, keepdims=True) + 1e-05  13.1 us
  transfers between devices with their start and end apart: 2, of which 1 were waited for; matrix products, arithmetic and copies ran while one was open for 14% of the time, Pallas kernels for 0%

profile of v1, /device:TPU:0, one launch (start us, length us, event | category | flops | bytes accessed | tf_op | source)
XLA Modules:
  0.0 279.2 jit_solution(5476236801310386444)
XLA Ops:
  7.2 0.0 copy-start
  7.2 0.0 all-gather.7.cloned.1.call-start
  7.2 0.7 all-gather.7.cloned.1.call-update
  7.9 2.2 stack.2
  10.1 7.5 %all-to-all-start = ((f32[16,384,64]{1,2,0:T(8,128)}), f32[16,384,64]{1,2,0:T(8,128)}, u32[]{:S(2)}, u32[]{:S(2)}) async-start(f32[16,384,64]{1,2,0:T(8,128)} %stack.2), calls=%async_computation | async-start | bytes 3145728 | tf_op jit(solution)/shard_map/all_to_all | solution.py:58
  17.6 5.9 %all_gather.28 = f32[48,1024]{1,0:T(8,128)S(1)} all-gather(f32[48,512]{1,0:T(8,128)} %param.14), channel_id=1, replica_groups=mesh['row'=16,'col'=2] {'col'}, dimensions={1}, use_global_device_ids=true | all-gather | bytes 294912 | tf_op jit(solution)/shard_map/all_gather | solution.py:54
  23.5 0.2 copy.49
  23.7 0.0 copy-start.7
  23.7 6.2 %reduce_sum.63 = f32[48,384]{1,0:T(8,128)S(1)} reduce(f32[48,384,128]{2,1,0:T(8,128)} %param.17, f32[]{:T(128)} %constant.13.clone.1), dimensions={2}, to_apply=%region_0.0 | reduce | flops 2340864 | bytes 9510916 | tf_op jit(solution)/shard_map/reduce_sum | solution.py:20
  29.9 7.7 %multiply_reduce_fusion.1 = f32[48,384]{1,0:T(8,128)S(1)} fusion(f32[48,384,128]{2,1,0:T(8,128)} %param.17, f32[48,384]{1,0:T(8,128)S(1)} %broadcast_multiply_fusion.1), kind=kLoop, calls=%fused_computation.12 | loop fusion | flops 7059456 | bytes 9584640 | tf_op jit(solution)/shard_map/reduce_sum | solution.py:21
  37.7 0.0 copy-done.7
  37.7 15.9 %fusion.9 = f32[48,384,32]{1,2,0:T(8,128)} fusion(f32[48,384,128]{2,1,0:T(8,128)} %param.17, f32[48,384]{1,0:T(8,128)S(1)} %add_rsqrt_fusion.1, f32[48,384]{1,0:T(8,128)S(1)} %broadcast_multiply_fusion.1, f32[128,32]{0,1:T(8,128)S(1)} %copy-done.7), kind=kOutput, calls=%fused_computation.10 | convolution fusion | flops 910688256 | bytes 11960320 | tf_op jit(solution)/shard_map/ijc,ch->ihj/dot_general | solution.py:53
  53.6 14.3 %all-gather.7.cloned.1.call-done = f32[384,1024]{0,1:T(8,128)} async-done(((f32[384,64]{0,1:T(8,128)}), f32[384,1024]{0,1:T(8,128)}) %all-gather.7.cloned.1.call-update) | async-done | bytes 1572880 | tf_op jit(solution)/shard_map/all_gather | solution.py:56
  67.9 5.7 %fusion.45 = (f32[48,32]{0,1:T(8,128)S(1)}, f32[48,32,384]{2,0,1:T(8,128)S(1)}) fusion(f32[48,384,32]{1,2,0:T(8,128)} %fusion.9, f32[384,32,32]{0,2,1:T(8,128)} %bitcast.73, f32[48,32,32]{0,2,1:T(8,128)S(1)} %bitcast.72), kind=kOutput, calls=%fused_computation.63 | convolution fusion | flops 228260352 | bytes 6494208 | tf_op jit(solution)/shard_map/ihd,jhd->ihj/dot_general | solution.py:34
  73.5 0.0 copy-start.2
  73.5 0.0 copy-start.4
  73.5 0.0 slice-start.6
  73.6 1.4 copy-done.2
  75.0 0.8 fusion.18
  75.8 0.0 all-to-all-done
  75.8 5.1 %fusion.20 = f32[48,32,32]{0,2,1:T(8,128)S(1)} fusion(f32[384,32,32]{0,2,1:T(8,128)} %bitcast.6, f32[48,32,384]{2,0,1:T(8,128)} %copy-done.2, f32[48,32]{0,1:T(8,128)S(1)} %get-tuple-element.37), kind=kOutput, calls=%fused_computation.22 | convolution fusion | flops 227082240 | bytes 4134912 | tf_op jit(solution)/shard_map/ihj,jhd->ihd/dot_general | solution.py:38
  80.9 4.4 %all-gather.3 = f32[2,48,32]{1,2,0:T(8,128)S(1)} all-gather(f32[1,48,32]{1,2,0:T(8,128)S(1)} %bitcast.74), channel_id=3, replica_groups=mesh['row'=16,'col'=2] {'col'}, dimensions={0}, use_global_device_ids=true | all-gather | bytes 18432 | tf_op jit(solution)/shard_map/all_gather | solution.py:10
  85.3 4.4 %all-gather.4 = f32[2,48,32]{1,2,0:T(8,128)S(1)} all-gather(f32[1,48,32]{1,2,0:T(8,128)S(1)} %bitcast.75), channel_id=4, replica_groups=mesh['row'=16,'col'=2] {'col'}, dimensions={0}, use_global_device_ids=true | all-gather | bytes 18432 | tf_op jit(solution)/shard_map/all_gather | solution.py:10
  89.7 0.1 copy.54
  89.8 0.1 copy.52
  89.8 0.7 copy.53
  90.5 0.7 copy.51
  91.2 0.0 copy-start.8
  91.2 18.0 %all-gather = f32[96,32,32]{2,1,0:T(8,128)S(1)} all-gather(f32[48,32,32]{2,1,0:T(8,128)S(1)} %copy.51), channel_id=2, replica_groups=mesh['row'=16,'col'=2] {'col'}, dimensions={0}, use_global_device_ids=true | all-gather | bytes 589824 | tf_op jit(solution)/shard_map/all_gather | solution.py:10
  109.3 2.0 fusion.23
  111.3 0.4 reshape.152
  111.7 0.0 copy-done
  111.7 2.3 fusion.42
  114.0 0.0 copy-start.3
  114.0 4.9 %all-reduce.1 = (f32[48]{0:T(128)S(1)}, f32[48]{0:T(128)S(1)}) all-reduce(f32[48]{0:T(128)S(1)} %get-tuple-element.19, f32[48]{0:T(128)S(1)} %get-tuple-element.18), channel_id=1, replica_groups=mesh['row'=16,'col'=2] {'col'}, use_global_device_ids=true, to_apply=%region_7.0 | all-reduce | flops 96 | bytes 768 | tf_op jit(solution)/shard_map/psum | solution.py:71
  119.0 1.2 fusion.24
  120.2 1.2 fusion.25
  121.4 8.6 %all-reduce = (f32[48,64]{1,0:T(8,128)S(1)}, f32[48,64]{1,0:T(8,128)S(1)}) all-reduce(f32[48,64]{1,0:T(8,128)S(1)} %fusion.24, f32[48,64]{1,0:T(8,128)S(1)} %fusion.25), channel_id=1, replica_groups=mesh['row'=16,'col'=2] {'col'}, use_global_device_ids=true, to_apply=%region_9.0 | all-reduce | flops 6144 | bytes 49152 | tf_op jit(solution)/shard_map/psum | solution.py:79
  130.0 0.0 copy-done.4
  130.0 0.2 fusion.32
  130.2 21.9 %all_gather.35 = f32[768,64]{1,0:T(8,128)S(1)} all-gather(f32[48,64]{1,0:T(8,128)S(1)} %get-tuple-element.20), channel_id=1, replica_groups=mesh['row'=16,'col'=2] {'row'}, dimensions={0}, use_global_device_ids=true | all-gather | bytes 208896 | tf_op jit(solution)/shard_map/all_gather | solution.py:80
  152.0 0.3 fusion.30
  152.3 0.0 slice-done.6
  152.4 22.6 %fusion.46 = (f32[48,384]{0,1:T(8,128)S(1)}, f32[48,384,128]{2,0,1:T(8,128)}) fusion(f32[128]{0:T(128)S(1)} %copy-done.8, f32[384,128]{1,0:T(8,128)S(1)} %fusion.30, f32[48,128]{1,0:T(8,128)S(1)} %fusion.32, f32[64,128]{1,0:T(8,128)S(1)} %slice-done.6, f32[384,64]{1,0:T(8,128)S(1)} %constant_dynamic-slice_fusion, f32[48,64]{1,0:T(8,128)S(1)} %get-tuple-element.21, ...), kind=kOutput, calls=%fused_computation.64 | convolution fusion | flops 1826863104 | bytes 19313152 | tf_op jit(solution)/shard_map/ip,jpc->ijc/dot_general | solution.py:89
  174.9 0.1 copy.57
  175.1 0.0 slice-start
  175.1 0.1 copy.58
  175.2 0.0 slice-start.1
  175.2 0.0 slice-start.2
  175.2 10.5 %copy.56 = f32[48,384,128]{2,1,0:T(8,128)} copy(f32[48,384,128]{2,0,1:T(8,128)} %get-tuple-element.41) | data formatting | bytes 18874368 | tf_op jit(solution)/shard_map/add | solution.py:94
  185.7 0.0 slice-done.2
  185.7 5.4 %multiply_reduce_fusion = f32[48,384]{0,1:T(8,128)S(1)} fusion(f32[48,384,128]{2,0,1:T(8,128)S(1)} %bitcast.67, f32[48,384]{0,1:T(8,128)S(1)} %copy.58), kind=kLoop, calls=%fused_computation.9 | loop fusion | flops 7059456 | bytes 9584640 | tf_op jit(solution)/shard_map/reduce_sum | solution.py:21
  191.2 0.1 copy.59
  191.3 0.0 copy-start.5
  191.3 0.0 slice-start.3
  191.3 11.4 %fusion.8 = f32[18432,128]{1,0:T(8,128)S(1)} fusion(f32[48,384,128]{2,1,0:T(8,128)} %copy.56, f32[18432]{0:T(1024)S(1)} %rsqrt.26, f32[18432]{0:T(1024)S(1)} %div.39), kind=kLoop, calls=%fused_computation.7 | loop fusion | flops 4718592 | bytes 19021824 | tf_op jit(solution)/shard_map/mul | solution.py:21
  202.7 0.0 copy-done.5
  202.8 0.0 slice-start.4
  202.8 0.0 slice-start.5
  202.8 0.0 copy-start.6
  202.8 33.8 %fusion.47 = f32[18432,512]{1,0:T(8,128)} fusion(f32[18432,128]{1,0:T(8,128)S(1)} %fusion.8, f32[128,512]{1,0:T(8,128)S(1)} %copy-done.5), kind=kOutput, calls=%fused_computation.65 | convolution fusion | flops 14495514624 | bytes 47448064 | tf_op jit(solution)/shard_map/dot_general | solution.py:96
  236.6 0.0 slice-done.3
  236.6 0.0 copy-start.1
  236.6 35.4 %fusion.2 = f32[18432,128]{1,0:T(8,128)} fusion(f32[18432,128]{1,0:T(8,128)S(1)} %bitcast.70, f32[512,128]{1,0:T(8,128)S(1)} %copy-done.6, f32[18432,512]{1,0:T(8,128)} %fusion.47), kind=kOutput, calls=%fused_computation.2 | convolution fusion | flops 14507311104 | bytes 56885248 | tf_op jit(solution)/shard_map/dot_general | solution.py:97
  (19 shorter events, 0.1 us)
Async XLA Ops:
  7.2 104.5 %copy-start = (f32[1024,512]{1,0:T(8,128)S(1)}, f32[1024,512]{1,0:T(8,128)}, u32[]{:S(2)}) copy-start(f32[1024,512]{1,0:T(8,128)} %param.19) | copy-start | bytes 6291460
  7.2 60.7 %all-gather.7.cloned.1.call-start = ((), (), s32[]{:S(2)}) async-start(), calls=%async_computation.1 | async-start | bytes 1671168 | tf_op jit(solution)/shard_map/all_gather | solution.py:56
  10.1 65.6 %all-to-all-start = ((f32[16,384,64]{1,2,0:T(8,128)}), f32[16,384,64]{1,2,0:T(8,128)}, u32[]{:S(2)}, u32[]{:S(2)}) async-start(f32[16,384,64]{1,2,0:T(8,128)} %stack.2), calls=%async_computation | async-start | bytes 3145728 | tf_op jit(solution)/shard_map/all_to_all | solution.py:58
  23.7 14.0 %copy-start.7 = (f32[128,32]{0,1:T(8,128)S(1)}, f32[128,32]{0,1:T(8,128)}, u32[]{:S(2)}) copy-start(f32[128,32]{0,1:T(8,128)} %param.18) | copy-start | bytes 49156
  73.5 1.4 copy-start.2
  73.5 56.4 %copy-start.4 = (f32[128,128]{1,0:T(8,128)S(1)}, f32[128,128]{1,0:T(8,128)}, u32[]{:S(2)}) copy-start(f32[128,128]{1,0:T(8,128)} %param.22) | copy-start | bytes 196612
  73.5 78.8 %slice-start.6 = ((f32[128,128]{1,0:T(8,128)}), f32[64,128]{1,0:T(8,128)S(1)}, s32[]{:S(2)}) async-start(f32[128,128]{1,0:T(8,128)} %param.22), calls=%async_computation.8 | async-start | bytes 65536 | tf_op jit(solution)/shard_map/slice | solution.py:83
  91.2 61.1 %copy-start.8 = (f32[128]{0:T(128)S(1)}, f32[128]{0:T(128)}, u32[]{:S(2)}) copy-start(f32[128]{0:T(128)} %param.23) | copy-start | bytes 1540
  114.0 60.9 %copy-start.3 = (f32[48,512]{1,0:T(8,128)}, f32[48,512]{1,0:T(8,128)S(1)}, u32[]{:S(2)}) copy-start(f32[48,512]{1,0:T(8,128)S(1)} %get-tuple-element.39) | copy-start | bytes 294916
  175.1 10.6 %slice-start = ((s8[9437184]{0:T(1024)(128)(4,1)}), s8[1048576]{0:T(1024)(128)(4,1)S(1)}, s32[]{:S(2)}) async-start(s8[9437184]{0:T(1024)(128)(4,1)} %bitcast.66), calls=%async_computation.2 | async-start | bytes 2097152
  175.2 10.5 %slice-start.1 = ((s8[9437184]{0:T(1024)(128)(4,1)}), s8[4194304]{0:T(1024)(128)(4,1)S(1)}, s32[]{:S(2)}) async-start(s8[9437184]{0:T(1024)(128)(4,1)} %bitcast.66), calls=%async_computation.3 | async-start | bytes 8388608
  175.2 10.5 %slice-start.2 = ((s8[9437184]{0:T(1024)(128)(4,1)}), s8[4194304]{0:T(1024)(128)(4,1)S(1)}, s32[]{:S(2)}) async-start(s8[9437184]{0:T(1024)(128)(4,1)} %bitcast.66), calls=%async_computation.4 | async-start | bytes 8388608
  191.3 11.4 %copy-start.5 = (f32[128,512]{1,0:T(8,128)S(1)}, f32[128,512]{1,0:T(8,128)}, u32[]{:S(2)}) copy-start(f32[128,512]{1,0:T(8,128)} %param.24) | copy-start | bytes 786436
  191.3 45.3 %slice-start.3 = ((s8[9437184]{0:T(1024)(128)(4,1)}), s8[4194304]{0:T(1024)(128)(4,1)S(1)}, s32[]{:S(2)}) async-start(s8[9437184]{0:T(1024)(128)(4,1)} %bitcast.68), calls=%async_computation.5 | async-start | bytes 8388608
  202.8 33.8 %slice-start.4 = ((s8[9437184]{0:T(1024)(128)(4,1)}), s8[4194304]{0:T(1024)(128)(4,1)S(1)}, s32[]{:S(2)}) async-start(s8[9437184]{0:T(1024)(128)(4,1)} %bitcast.68), calls=%async_computation.6 | async-start | bytes 8388608
  202.8 33.8 %slice-start.5 = ((s8[9437184]{0:T(1024)(128)(4,1)}), s8[1048576]{0:T(1024)(128)(4,1)S(1)}, s32[]{:S(2)}) async-start(s8[9437184]{0:T(1024)(128)(4,1)} %bitcast.68), calls=%async_computation.7 | async-start | bytes 2097152
  202.8 33.8 %copy-start.6 = (f32[512,128]{1,0:T(8,128)S(1)}, f32[512,128]{1,0:T(8,128)}, u32[]{:S(2)}) copy-start(f32[512,128]{1,0:T(8,128)} %param.25) | copy-start | bytes 786436
  236.6 35.5 %copy-start.1 = (f32[1024,512]{1,0:T(8,128)S(1)}, f32[1024,512]{1,0:T(8,128)}, u32[]{:S(2)}) copy-start(f32[1024,512]{1,0:T(8,128)} %param.19) | copy-start | bytes 6291460
Sparse Core Ops, SparseCore 0:
  10.3 57.5 all-gather.6
